TPU v7x, 32 devices: a whole 2x2x4 slice. The times are simulated.
32 devices in a mesh: member: 8 (over z, core), dp: 4 (over y, x).
Axes of the slice: x: 2, y: 2, z: 4, core: 2. Of those that a mesh axis runs over, the one named last changes fastest.
Arguments:
- feats: bfloat16 [8, 2048, 1024], P('member', 'dp'), may hold values from -160 to 160
- pair_weight: float32 [8, 3], replicated, may hold values from 0.5 to 2
Outputs:
- grad_centred: float32 [8, 2048, 1024], P('member', 'dp')
- cka: float32 [8, 3], P('member')
All inputs are finite; a program needn't handle non-finite values.
Results may differ from a plain program's by a relative error of at most 0.0053.
Values may be sent and summed in bfloat16 or wider, within the bound.
A program may use at most 128 MiB of HBM per device.

v0:
```python
import math
import jax
import jax.numpy as jnp
from jax import lax
from jax.sharding import PartitionSpec as P


def mixing(self_hsic, pair_hsic, pair_weight):
    pairs = pair_weight.shape[1]
    members = pair_weight.shape[0]
    partner_self = jnp.stack([jnp.roll(self_hsic, -o) for o in range(1, pairs + 1)], axis=1)
    norms = jnp.sqrt(self_hsic[:, None] * partner_self)
    cka = pair_hsic / norms
    weighted = pair_weight * cka
    incoming = sum((jnp.roll(weighted[:, o - 1], o) for o in range(1, pairs + 1)))
    self_coef = (jnp.sum(weighted, axis=1) + incoming) / (self_hsic + 1e-06)
    coef = 2.0 * pair_weight / norms
    eye = jnp.eye(members, dtype=jnp.float32)
    mix = -2.0 * self_coef[:, None] * eye
    for o in range(1, pairs + 1):
        ahead = coef[:, o - 1][:, None] * jnp.roll(eye, o, axis=1)
        mix = mix + ahead + ahead.T
    return (cka, mix)


def shards(feats, pair_weight):
    rows = feats[0]
    members = lax.axis_size("member")
    pairs = pair_weight.shape[1]
    whole = lax.all_gather(rows, "dp", axis=0, tiled=True)
    batch, width = whole.shape
    mean = jnp.sum(whole.astype(jnp.float32), axis=0) / batch
    centred = (whole.astype(jnp.float32) - mean).astype(jnp.bfloat16)
    own = (rows.astype(jnp.float32) - mean).astype(jnp.bfloat16)
    blocks = centred.reshape(members, batch // members, width)
    gram = jnp.einsum("rf,mcf->mrc", own, blocks, preferred_element_type=jnp.float32)
    held = lax.all_to_all(gram.astype(jnp.bfloat16), "member", 0, 0)
    held = held.astype(jnp.float32)
    sums = []
    for o in range(pairs + 1):
        sums.append(jnp.sum(held * jnp.roll(held, -o, axis=0), axis=(1, 2)))
    sums = lax.psum(jnp.stack(sums, axis=1), ("member", "dp"))
    cka, mix = mixing(sums[:, 0], sums[:, 1:], pair_weight)
    mixed = jnp.stack(
        [sum((mix[m, q] * held[q] for q in range(members))) for m in range(members)]
    ).astype(jnp.bfloat16)
    mixed = lax.all_to_all(mixed, "member", 0, 0)
    grad = jnp.einsum("jrc,jcf->rf", mixed, blocks, preferred_element_type=jnp.float32)
    grad = math.sqrt(batch) * grad
    own_cka = lax.dynamic_slice_in_dim(cka, lax.axis_index("member"), 1, axis=0)
    return (grad[None], own_cka)


def solution(mesh):
    return jax.shard_map(
        shards,
        mesh=mesh,
        in_specs=(P("member", "dp", None), P()),
        out_specs=(P("member", "dp", None), P("member", None)),
        check_vma=False,
    )
```

profile of v0, /device:TPU:0, one launch (start us, length us, event | category | flops | bytes accessed | tf_op | source)
XLA Modules:
  0.0 292.4 jit_solution(5384150362921916437)
XLA Ops:
  7.2 0.0 all-gather.3.cloned.1.call-start
  7.2 0.7 all-gather.3.cloned.1.call-update
  7.9 57.2 %all-gather.3.cloned.1.call-done = bf16[1,2048,1024]{2,1,0:T(8,128)(2,1)} async-done(((bf16[1,512,1024]{2,1,0:T(8,128)(2,1)}), bf16[1,2048,1024]{2,1,0:T(8,128)(2,1)}) %all-gather.3.cloned.1.call-update) | async-done | bytes 4194320 | tf_op jit(solution)/shard_map/all_gather | solution.py:30
  65.1 0.0 copy-start.1
  65.1 3.0 %convert_reduce_fusion = f32[1024]{0:T(1024)S(1)} fusion(bf16[1,2048,1024]{2,1,0:T(8,128)(2,1)} %all-gather.3.cloned.1.call-done), kind=kLoop, calls=%fused_computation | loop fusion | flops 4193280 | bytes 4198400 | tf_op jit(solution)/shard_map/reduce_sum | solution.py:32
  68.2 0.4 copy-done.1
  68.6 1.3 fusion.1
  69.9 0.0 copy-start
  69.9 1.9 copy-done
  71.8 0.0 copy-done.2
  71.8 3.8 %convert_bitcast_fusion.1 = bf16[8,512,256]{1,2,0:T(8,128)(2,1)} fusion(bf16[8,256,1024]{2,1,0:T(8,128)(2,1)S(1)} %bitcast.136, bf16[1,512,1024]{2,1,0:T(8,128)(2,1)S(1)} %copy-done.2, f32[1024]{0:T(1024)S(1)} %broadcast_multiply_fusion), kind=kOutput, calls=%fused_computation.13 | convolution fusion | flops 2150105088 | bytes 7344128 | tf_op jit(solution)/shard_map/rf,mcf->mrc/dot_general | solution.py:36
  75.5 4.6 %all-to-all-start = ((bf16[8,512,256]{1,2,0:T(8,128)(2,1)}), bf16[8,512,256]{1,2,0:T(8,128)(2,1)S(1)}, u32[]{:S(2)}, u32[]{:S(2)}) async-start(bf16[8,512,256]{1,2,0:T(8,128)(2,1)} %convert_bitcast_fusion.1), calls=%async_computation | async-start | bytes 4194304 | tf_op jit(solution)/shard_map/all_to_all | solution.py:37
  80.1 0.1 slice.447
  80.2 0.1 slice.450
  80.3 0.1 slice.453
  80.4 0.1 copy.13
  80.4 0.1 copy.14
  80.5 48.6 %all-to-all-done = bf16[8,512,256]{1,2,0:T(8,128)(2,1)S(1)} async-done(((bf16[8,512,256]{1,2,0:T(8,128)(2,1)}), bf16[8,512,256]{1,2,0:T(8,128)(2,1)S(1)}, u32[]{:S(2)}, u32[]{:S(2)}) %all-to-all-start) | async-done | bytes 2097184 | tf_op jit(solution)/shard_map/all_to_all | solution.py:37
  129.2 0.5 slice.526
  129.7 0.4 slice.528
  130.1 0.4 slice.530
  130.5 0.2 slice.531
  130.7 0.1 slice.529
  130.8 0.1 slice.527
  130.9 0.0 copy-start.3
  130.9 1.8 multiply_reduce_fusion
  132.7 0.1 copy.4
  132.8 37.0 %psum.7 = f32[8,4]{0,1:T(4,128)S(1)} all-reduce(f32[8,4]{0,1:T(4,128)S(1)} %pad_maximum_fusion), channel_id=1, replica_groups=mesh['member'=8,'dp'=4] {'member','dp'}, use_global_device_ids=true, to_apply=%region_5.6 | all-reduce | flops 32 | bytes 256 | tf_op jit(solution)/shard_map/psum | solution.py:42
  169.8 0.5 slice.430
  170.3 0.1 slice_bitcast_fusion.7
  170.4 0.1 slice_bitcast_fusion.6
  170.4 0.1 slice_bitcast_fusion.4
  170.5 0.7 maximum_bitcast_fusion
  171.2 0.1 maximum_bitcast_fusion.1
  171.3 0.1 maximum_bitcast_fusion.2
  171.4 0.0 copy-done.3
  171.4 0.6 slice.440
  172.0 0.1 slice.442
  172.1 0.1 slice.444
  172.2 0.7 slice_bitcast_fusion.1
  172.9 0.1 copy.7
  173.0 0.1 fusion.18
  173.0 0.1 copy.8
  173.1 0.1 maximum_multiply_fusion.5
  173.2 0.1 copy.9
  173.3 0.1 bitcast_add_fusion
  173.3 0.7 fusion.26
  174.1 0.6 fusion.27
  174.7 0.7 fusion.25
  175.4 0.7 fusion.24
  176.1 0.6 convert_element_type.47
  176.7 6.4 %fusion.9 = bf16[8,512,256]{1,2,0:T(8,128)(2,1)} fusion(f32[8,512,256]{1,2,0:T(8,128)S(1)} %convert_element_type.47, f32[]{:T(128)} %bitcast.34, f32[]{:T(128)} %bitcast.33, f32[]{:T(128)} %bitcast.32, f32[]{:T(128)} %bitcast.31, f32[]{:T(128)} %bitcast.30, f32[]{:T(128)} %bitcast.29, f32[]{:T(128)} %bitcast.28, f32[]{:T(128)} %bitcast.27), kind=kLoop, calls=%fused_computation.25 | loop fusion | flops 2097151 | bytes 4456480
  183.1 6.1 %fusion.10 = bf16[8,512,256]{1,2,0:T(8,128)(2,1)} fusion(bf16[8,512,256]{1,2,0:T(8,128)(2,1)} %fusion.9, f32[8,512,256]{1,2,0:T(8,128)S(1)} %convert_element_type.47, f32[]{:T(128)} %bitcast.42, f32[]{:T(128)} %bitcast.41, f32[]{:T(128)} %bitcast.40, f32[]{:T(128)} %bitcast.39, f32[]{:T(128)} %bitcast.38, f32[]{:T(128)} %bitcast.37, f32[]{:T(128)} %bitcast.36, ...), kind=kLoop, calls=%fused_computation.26 | loop fusion | flops 2097152 | bytes 4460544
  189.2 6.1 %fusion.11 = bf16[8,512,256]{1,2,0:T(8,128)(2,1)} fusion(bf16[8,512,256]{1,2,0:T(8,128)(2,1)} %fusion.10, f32[8,512,256]{1,2,0:T(8,128)S(1)} %convert_element_type.47, f32[]{:T(128)} %bitcast.50, f32[]{:T(128)} %bitcast.49, f32[]{:T(128)} %bitcast.48, f32[]{:T(128)} %bitcast.47, f32[]{:T(128)} %bitcast.46, f32[]{:T(128)} %bitcast.45, f32[]{:T(128)} %bitcast.44, ...), kind=kLoop, calls=%fused_computation.27 | loop fusion | flops 2097152 | bytes 4460544
  195.3 6.1 %fusion.12 = bf16[8,512,256]{1,2,0:T(8,128)(2,1)} fusion(bf16[8,512,256]{1,2,0:T(8,128)(2,1)} %fusion.11, f32[8,512,256]{1,2,0:T(8,128)S(1)} %convert_element_type.47, f32[]{:T(128)} %bitcast.58, f32[]{:T(128)} %bitcast.57, f32[]{:T(128)} %bitcast.56, f32[]{:T(128)} %bitcast.55, f32[]{:T(128)} %bitcast.54, f32[]{:T(128)} %bitcast.53, f32[]{:T(128)} %bitcast.52, ...), kind=kLoop, calls=%fused_computation.28 | loop fusion | flops 2097152 | bytes 4460544
  201.4 6.3 %fusion.13 = bf16[8,512,256]{1,2,0:T(8,128)(2,1)} fusion(bf16[8,512,256]{1,2,0:T(8,128)(2,1)} %fusion.12, f32[8,512,256]{1,2,0:T(8,128)S(1)} %convert_element_type.47, f32[]{:T(128)} %bitcast.66, f32[]{:T(128)} %bitcast.65, f32[]{:T(128)} %bitcast.64, f32[]{:T(128)} %bitcast.63, f32[]{:T(128)} %bitcast.62, f32[]{:T(128)} %bitcast.61, f32[]{:T(128)} %bitcast.60, ...), kind=kLoop, calls=%fused_computation.29 | loop fusion | flops 2097152 | bytes 4460544
  207.7 6.2 %fusion.14 = bf16[8,512,256]{1,2,0:T(8,128)(2,1)} fusion(bf16[8,512,256]{1,2,0:T(8,128)(2,1)} %fusion.13, f32[8,512,256]{1,2,0:T(8,128)S(1)} %convert_element_type.47, f32[]{:T(128)} %bitcast.74, f32[]{:T(128)} %bitcast.73, f32[]{:T(128)} %bitcast.72, f32[]{:T(128)} %bitcast.71, f32[]{:T(128)} %bitcast.70, f32[]{:T(128)} %bitcast.69, f32[]{:T(128)} %bitcast.68, ...), kind=kLoop, calls=%fused_computation.30 | loop fusion | flops 2097152 | bytes 4460544
  214.0 6.2 %fusion.15 = bf16[8,512,256]{1,2,0:T(8,128)(2,1)} fusion(bf16[8,512,256]{1,2,0:T(8,128)(2,1)} %fusion.14, f32[8,512,256]{1,2,0:T(8,128)S(1)} %convert_element_type.47, f32[]{:T(128)} %bitcast.82, f32[]{:T(128)} %bitcast.81, f32[]{:T(128)} %bitcast.80, f32[]{:T(128)} %bitcast.79, f32[]{:T(128)} %bitcast.78, f32[]{:T(128)} %bitcast.77, f32[]{:T(128)} %bitcast.76, ...), kind=kLoop, calls=%fused_computation.31 | loop fusion | flops 2097152 | bytes 4460544
  220.2 6.2 %fusion.16 = bf16[8,512,256]{1,2,0:T(8,128)(2,1)} fusion(bf16[8,512,256]{1,2,0:T(8,128)(2,1)} %fusion.15, f32[8,512,256]{1,2,0:T(8,128)S(1)} %convert_element_type.47, f32[]{:T(128)} %bitcast.90, f32[]{:T(128)} %bitcast.89, f32[]{:T(128)} %bitcast.88, f32[]{:T(128)} %bitcast.87, f32[]{:T(128)} %bitcast.86, f32[]{:T(128)} %bitcast.85, f32[]{:T(128)} %bitcast.84, ...), kind=kLoop, calls=%fused_computation.32 | loop fusion | flops 2097152 | bytes 4460544 | tf_op jit(solution)/shard_map/stack | solution.py:44
  226.4 4.2 %all-to-all-start.1 = ((bf16[8,512,256]{1,2,0:T(8,128)(2,1)}), bf16[8,512,256]{1,2,0:T(8,128)(2,1)S(1)}, u32[]{:S(2)}, u32[]{:S(2)}) async-start(bf16[8,512,256]{1,2,0:T(8,128)(2,1)} %fusion.16), calls=%async_computation.1 | async-start | bytes 4194304 | tf_op jit(solution)/shard_map/all_to_all | solution.py:47
  230.6 0.1 constant_dynamic-slice_fusion
  230.7 0.6 copy.11
  231.3 48.4 %all-to-all-done.1 = bf16[8,512,256]{1,2,0:T(8,128)(2,1)S(1)} async-done(((bf16[8,512,256]{1,2,0:T(8,128)(2,1)}), bf16[8,512,256]{1,2,0:T(8,128)(2,1)S(1)}, u32[]{:S(2)}, u32[]{:S(2)}) %all-to-all-start.1) | async-done | bytes 2097184 | tf_op jit(solution)/shard_map/all_to_all | solution.py:47
  279.7 5.9 %fusion.5 = f32[1,512,1024]{2,1,0:T(8,128)} fusion(bf16[8,512,256]{1,2,0:T(8,128)(2,1)S(1)} %all-to-all-done.1, bf16[8,256,1024]{2,1,0:T(8,128)(2,1)} %bitcast.137), kind=kOutput, calls=%fused_computation.12 | convolution fusion | flops 2148007936 | bytes 8388608 | tf_op jit(solution)/shard_map/jrc,jcf->rf/dot_general | solution.py:48
  (13 shorter events, 0.1 us)
Async XLA Ops:
  7.2 58.0 %all-gather.3.cloned.1.call-start = ((), (), s32[]{:S(2)}) async-start(), calls=%async_computation.2 | async-start | bytes 5242880 | tf_op jit(solution)/shard_map/all_gather | solution.py:30
  65.1 3.4 %copy-start.1 = (bf16[1,2048,1024]{2,1,0:T(8,128)(2,1)S(1)}, bf16[1,2048,1024]{2,1,0:T(8,128)(2,1)}, u32[]{:S(2)}) copy-start(bf16[1,2048,1024]{2,1,0:T(8,128)(2,1)} %all-gather.3.cloned.1.call-done) | copy-start | bytes 12582916
  68.6 3.2 %copy-start.2 = (bf16[1,512,1024]{2,1,0:T(8,128)(2,1)S(1)}, bf16[1,512,1024]{2,1,0:T(8,128)(2,1)}, u32[]{:S(2)}) copy-start(bf16[1,512,1024]{2,1,0:T(8,128)(2,1)} %param.2) | copy-start | bytes 3145732
  69.9 1.9 copy-start
  75.5 53.6 %all-to-all-start = ((bf16[8,512,256]{1,2,0:T(8,128)(2,1)}), bf16[8,512,256]{1,2,0:T(8,128)(2,1)S(1)}, u32[]{:S(2)}, u32[]{:S(2)}) async-start(bf16[8,512,256]{1,2,0:T(8,128)(2,1)} %convert_bitcast_fusion.1), calls=%async_computation | async-start | bytes 4194304 | tf_op jit(solution)/shard_map/all_to_all | solution.py:37
  130.9 40.5 %copy-start.3 = (f32[8,3]{0,1:T(4,128)S(1)}, f32[8,3]{0,1:T(4,128)}, u32[]{:S(2)}) copy-start(f32[8,3]{0,1:T(4,128)} %param.3) | copy-start | bytes 292
  226.4 53.3 %all-to-all-start.1 = ((bf16[8,512,256]{1,2,0:T(8,128)(2,1)}), bf16[8,512,256]{1,2,0:T(8,128)(2,1)S(1)}, u32[]{:S(2)}, u32[]{:S(2)}) async-start(bf16[8,512,256]{1,2,0:T(8,128)(2,1)} %fusion.16), calls=%async_computation.1 | async-start | bytes 4194304 | tf_op jit(solution)/shard_map/all_to_all | solution.py:47
Sparse Core Ops, SparseCore 0:
  9.8 55.2 all-gather.2
where the time goes:
time: 293 us; the launch traced here: 292 us
  waiting for transfers between devices  155 us (53%)
  other arithmetic  58.2 us (20%)
  blocking collectives  37 us (13%)
  between operations  14.1 us (5%)
  local copies, waits for them, and re-layouts  9.6 us (3%)
  matrix products  9.6 us (3%)
  starting transfers between devices  8.86 us (3%)
    all_gather x1, waiting for transfers between devices, shards(): whole = lax.all_gather(rows, 'dp', axis=0, tiled=True)  57.2 us
    all_to_all x1, waiting for transfers between devices, shards(): held = lax.all_to_all(gram.astype(jnp.bfloat16), 'member', 0, 0)  48.6 us
    all_to_all x1, waiting for transfers between devices, shards(): mixed = lax.all_to_all(mixed, 'member', 0, 0)  48.4 us
    unnamed x7, other arithmetic  43.5 us
    psum x1, blocking collectives, shards(): sums = lax.psum(jnp.stack(sums, axis=1), ('member', 'dp'))  37 us
    another operation x1, other arithmetic, shards(): jnp.stack([sum((mix[m, q] * held[q] for q in range(members))) for m in ra...  6.23 us
  transfers between devices with their start and end apart: 3, of which 3 were waited for; matrix products, arithmetic and copies ran while one was open for 0% of the time, Pallas kernels for 0%

commit v1 on v0

--- a/solution.py
+++ b/solution.py
@@ -39,7 +39,7 @@
     sums = []
     for o in range(pairs + 1):
         sums.append(jnp.sum(held * jnp.roll(held, -o, axis=0), axis=(1, 2)))
-    sums = lax.psum(jnp.stack(sums, axis=1), ("member", "dp"))
+    sums = jnp.sum(lax.all_gather(jnp.stack(sums, axis=1), ("member", "dp")), axis=0)
     cka, mix = mixing(sums[:, 0], sums[:, 1:], pair_weight)
     mixed = jnp.stack(
         [sum((mix[m, q] * held[q] for q in range(members))) for m in range(members)]

time: 293 us -> 321 us (1.096)
  blocking collectives: 37 us -> 65.6 us
    all_gather x0 -> x1, blocking collectives: none -> 65.6 us  [shards(): lax.all_gather(jnp.stack(sums, axis=1), ('member', 'dp'))]
    psum x1 -> x0, blocking collectives: 37 us -> none  [shards(): sums = lax.psum(jnp.stack(sums, axis=1), ('member', 'dp'))]
    unnamed x7 -> x8, other arithmetic: 43.5 us -> 43.5 us
where the time goes in v1:
time: 321 us; the launch traced here: 320 us
  waiting for transfers between devices  155 us (48%)
  blocking collectives  65.6 us (20%)
  other arithmetic  58.3 us (18%)
  between operations  14.2 us (4%)
  local copies, waits for them, and re-layouts  9.61 us (3%)
  matrix products  9.6 us (3%)
  starting transfers between devices  8.25 us (3%)
    all_gather x1, blocking collectives, shards(): lax.all_gather(jnp.stack(sums, axis=1), ('member', 'dp'))  65.6 us
    all_gather x1, waiting for transfers between devices, shards(): whole = lax.all_gather(rows, 'dp', axis=0, tiled=True)  57.2 us
    all_to_all x1, waiting for transfers between devices, shards(): held = lax.all_to_all(gram.astype(jnp.bfloat16), 'member', 0, 0)  48.6 us
    all_to_all x1, waiting for transfers between devices, shards(): mixed = lax.all_to_all(mixed, 'member', 0, 0)  48.3 us
    unnamed x8, other arithmetic  43.5 us
  transfers between devices with their start and end apart: 3, of which 3 were waited for; matrix products, arithmetic and copies ran while one was open for 0% of the time, Pallas kernels for 0%

profile of v1, /device:TPU:0, one launch (start us, length us, event | category | flops | bytes accessed | tf_op | source)
XLA Modules:
  0.0 320.3 jit_solution(15895080958092633944)
XLA Ops:
  7.2 0.0 all-gather.5.cloned.1.call-start
  7.2 0.7 all-gather.5.cloned.1.call-update
  7.9 57.2 %all-gather.5.cloned.1.call-done = bf16[1,2048,1024]{2,1,0:T(8,128)(2,1)} async-done(((bf16[1,512,1024]{2,1,0:T(8,128)(2,1)}), bf16[1,2048,1024]{2,1,0:T(8,128)(2,1)}) %all-gather.5.cloned.1.call-update) | async-done | bytes 4194320 | tf_op jit(solution)/shard_map/all_gather | solution.py:30
  65.1 0.0 copy-start.1
  65.1 3.0 convert_reduce_fusion
  68.2 0.4 copy-done.1
  68.6 1.3 fusion.1
  69.9 0.0 copy-start
  69.9 1.9 copy-done
  71.8 0.0 copy-done.2
  71.8 3.8 %convert_bitcast_fusion.1 = bf16[8,512,256]{1,2,0:T(8,128)(2,1)} fusion(bf16[8,256,1024]{2,1,0:T(8,128)(2,1)S(1)} %bitcast.138, bf16[1,512,1024]{2,1,0:T(8,128)(2,1)S(1)} %copy-done.2, f32[1024]{0:T(1024)S(1)} %broadcast_multiply_fusion), kind=kOutput, calls=%fused_computation.13 | convolution fusion | flops 2150105088 | bytes 7344128 | tf_op jit(solution)/shard_map/rf,mcf->mrc/dot_general | solution.py:36
  75.5 4.6 %all-to-all-start = ((bf16[8,512,256]{1,2,0:T(8,128)(2,1)}), bf16[8,512,256]{1,2,0:T(8,128)(2,1)S(1)}, u32[]{:S(2)}, u32[]{:S(2)}) async-start(bf16[8,512,256]{1,2,0:T(8,128)(2,1)} %convert_bitcast_fusion.1), calls=%async_computation | async-start | bytes 4194304 | tf_op jit(solution)/shard_map/all_to_all | solution.py:37
  80.1 0.1 slice.447
  80.2 0.1 slice.450
  80.3 0.1 slice.453
  80.4 0.1 copy.21
  80.4 0.1 copy.22
  80.5 0.1 copy.12
  80.6 48.6 %all-to-all-done = bf16[8,512,256]{1,2,0:T(8,128)(2,1)S(1)} async-done(((bf16[8,512,256]{1,2,0:T(8,128)(2,1)}), bf16[8,512,256]{1,2,0:T(8,128)(2,1)S(1)}, u32[]{:S(2)}, u32[]{:S(2)}) %all-to-all-start) | async-done | bytes 2097184 | tf_op jit(solution)/shard_map/all_to_all | solution.py:37
  129.2 0.5 slice.526
  129.7 0.4 slice.528
  130.1 0.4 slice.530
  130.5 0.2 slice.531
  130.7 0.1 slice.529
  130.8 0.1 slice.527
  130.9 0.0 copy-start.3
  130.9 1.8 multiply_reduce_fusion
  132.7 65.6 %all-gather.2 = f32[32,8,4]{1,2,0:T(4,128)S(1)} all-gather(f32[1,8,4]{1,2,0:T(4,128)S(1)} %maximum_bitcast_fusion), channel_id=3, replica_groups=mesh['member'=8,'dp'=4] {'member','dp'}, dimensions={0}, use_global_device_ids=true | all-gather | bytes 4224 | tf_op jit(solution)/shard_map/all_gather | solution.py:42
  198.4 0.5 slice.430
  198.9 0.1 slice_bitcast_fusion.7
  199.0 0.1 slice_bitcast_fusion.6
  199.1 0.1 slice_bitcast_fusion.4
  199.1 0.7 maximum_bitcast_fusion.1
  199.9 0.1 maximum_bitcast_fusion.2
  199.9 0.1 maximum_bitcast_fusion.3
  200.0 0.0 copy-done.3
  200.0 0.6 slice.440
  200.6 0.1 slice.442
  200.7 0.1 slice.444
  200.8 0.7 slice_bitcast_fusion.1
  201.5 0.1 copy.15
  201.6 0.1 fusion.18
  201.7 0.1 copy.16
  201.8 0.1 maximum_multiply_fusion.5
  201.8 0.1 copy.17
  201.9 0.1 bitcast_add_fusion
  202.0 0.7 fusion.26
  202.7 0.6 fusion.27
  203.3 0.7 fusion.25
  204.0 0.7 fusion.24
  204.8 0.6 convert_element_type.47
  205.3 6.4 %fusion.9 = bf16[8,512,256]{1,2,0:T(8,128)(2,1)} fusion(f32[8,512,256]{1,2,0:T(8,128)S(1)} %convert_element_type.47, f32[]{:T(128)} %bitcast.35, f32[]{:T(128)} %bitcast.34, f32[]{:T(128)} %bitcast.33, f32[]{:T(128)} %bitcast.32, f32[]{:T(128)} %bitcast.31, f32[]{:T(128)} %bitcast.30, f32[]{:T(128)} %bitcast.29, f32[]{:T(128)} %bitcast.28), kind=kLoop, calls=%fused_computation.25 | loop fusion | flops 2097151 | bytes 4456480
  211.7 6.1 %fusion.10 = bf16[8,512,256]{1,2,0:T(8,128)(2,1)} fusion(bf16[8,512,256]{1,2,0:T(8,128)(2,1)} %fusion.9, f32[8,512,256]{1,2,0:T(8,128)S(1)} %convert_element_type.47, f32[]{:T(128)} %bitcast.43, f32[]{:T(128)} %bitcast.42, f32[]{:T(128)} %bitcast.41, f32[]{:T(128)} %bitcast.40, f32[]{:T(128)} %bitcast.39, f32[]{:T(128)} %bitcast.38, f32[]{:T(128)} %bitcast.37, ...), kind=kLoop, calls=%fused_computation.26 | loop fusion | flops 2097152 | bytes 4460544
  217.8 6.1 %fusion.11 = bf16[8,512,256]{1,2,0:T(8,128)(2,1)} fusion(bf16[8,512,256]{1,2,0:T(8,128)(2,1)} %fusion.10, f32[8,512,256]{1,2,0:T(8,128)S(1)} %convert_element_type.47, f32[]{:T(128)} %bitcast.51, f32[]{:T(128)} %bitcast.50, f32[]{:T(128)} %bitcast.49, f32[]{:T(128)} %bitcast.48, f32[]{:T(128)} %bitcast.47, f32[]{:T(128)} %bitcast.46, f32[]{:T(128)} %bitcast.45, ...), kind=kLoop, calls=%fused_computation.27 | loop fusion | flops 2097152 | bytes 4460544
  224.0 6.1 %fusion.12 = bf16[8,512,256]{1,2,0:T(8,128)(2,1)} fusion(bf16[8,512,256]{1,2,0:T(8,128)(2,1)} %fusion.11, f32[8,512,256]{1,2,0:T(8,128)S(1)} %convert_element_type.47, f32[]{:T(128)} %bitcast.59, f32[]{:T(128)} %bitcast.58, f32[]{:T(128)} %bitcast.57, f32[]{:T(128)} %bitcast.56, f32[]{:T(128)} %bitcast.55, f32[]{:T(128)} %bitcast.54, f32[]{:T(128)} %bitcast.53, ...), kind=kLoop, calls=%fused_computation.28 | loop fusion | flops 2097152 | bytes 4460544
  230.0 6.3 %fusion.13 = bf16[8,512,256]{1,2,0:T(8,128)(2,1)} fusion(bf16[8,512,256]{1,2,0:T(8,128)(2,1)} %fusion.12, f32[8,512,256]{1,2,0:T(8,128)S(1)} %convert_element_type.47, f32[]{:T(128)} %bitcast.67, f32[]{:T(128)} %bitcast.66, f32[]{:T(128)} %bitcast.65, f32[]{:T(128)} %bitcast.64, f32[]{:T(128)} %bitcast.63, f32[]{:T(128)} %bitcast.62, f32[]{:T(128)} %bitcast.61, ...), kind=kLoop, calls=%fused_computation.29 | loop fusion | flops 2097152 | bytes 4460544
  236.4 6.2 %fusion.14 = bf16[8,512,256]{1,2,0:T(8,128)(2,1)} fusion(bf16[8,512,256]{1,2,0:T(8,128)(2,1)} %fusion.13, f32[8,512,256]{1,2,0:T(8,128)S(1)} %convert_element_type.47, f32[]{:T(128)} %bitcast.75, f32[]{:T(128)} %bitcast.74, f32[]{:T(128)} %bitcast.73, f32[]{:T(128)} %bitcast.72, f32[]{:T(128)} %bitcast.71, f32[]{:T(128)} %bitcast.70, f32[]{:T(128)} %bitcast.69, ...), kind=kLoop, calls=%fused_computation.30 | loop fusion | flops 2097152 | bytes 4460544
  242.6 6.2 %fusion.15 = bf16[8,512,256]{1,2,0:T(8,128)(2,1)} fusion(bf16[8,512,256]{1,2,0:T(8,128)(2,1)} %fusion.14, f32[8,512,256]{1,2,0:T(8,128)S(1)} %convert_element_type.47, f32[]{:T(128)} %bitcast.83, f32[]{:T(128)} %bitcast.82, f32[]{:T(128)} %bitcast.81, f32[]{:T(128)} %bitcast.80, f32[]{:T(128)} %bitcast.79, f32[]{:T(128)} %bitcast.78, f32[]{:T(128)} %bitcast.77, ...), kind=kLoop, calls=%fused_computation.31 | loop fusion | flops 2097152 | bytes 4460544
  248.8 6.2 %fusion.16 = bf16[8,512,256]{1,2,0:T(8,128)(2,1)} fusion(bf16[8,512,256]{1,2,0:T(8,128)(2,1)} %fusion.15, f32[8,512,256]{1,2,0:T(8,128)S(1)} %convert_element_type.47, f32[]{:T(128)} %bitcast.91, f32[]{:T(128)} %bitcast.90, f32[]{:T(128)} %bitcast.89, f32[]{:T(128)} %bitcast.88, f32[]{:T(128)} %bitcast.87, f32[]{:T(128)} %bitcast.86, f32[]{:T(128)} %bitcast.85, ...), kind=kLoop, calls=%fused_computation.32 | loop fusion | flops 2097152 | bytes 4460544 | tf_op jit(solution)/shard_map/stack | solution.py:44
  255.0 3.6 %all-to-all-start.1 = ((bf16[8,512,256]{1,2,0:T(8,128)(2,1)}), bf16[8,512,256]{1,2,0:T(8,128)(2,1)S(1)}, u32[]{:S(2)}, u32[]{:S(2)}) async-start(bf16[8,512,256]{1,2,0:T(8,128)(2,1)} %fusion.16), calls=%async_computation.1 | async-start | bytes 4194304 | tf_op jit(solution)/shard_map/all_to_all | solution.py:47
  258.7 0.1 constant_dynamic-slice_fusion
  258.7 0.6 copy.19
  259.3 48.3 %all-to-all-done.1 = bf16[8,512,256]{1,2,0:T(8,128)(2,1)S(1)} async-done(((bf16[8,512,256]{1,2,0:T(8,128)(2,1)}), bf16[8,512,256]{1,2,0:T(8,128)(2,1)S(1)}, u32[]{:S(2)}, u32[]{:S(2)}) %all-to-all-start.1) | async-done | bytes 2097184 | tf_op jit(solution)/shard_map/all_to_all | solution.py:47
  307.6 5.9 %fusion.5 = f32[1,512,1024]{2,1,0:T(8,128)} fusion(bf16[8,512,256]{1,2,0:T(8,128)(2,1)S(1)} %all-to-all-done.1, bf16[8,256,1024]{2,1,0:T(8,128)(2,1)} %bitcast.139), kind=kOutput, calls=%fused_computation.12 | convolution fusion | flops 2148007936 | bytes 8388608 | tf_op jit(solution)/shard_map/jrc,jcf->rf/dot_general | solution.py:48
  (14 shorter events, 0.1 us)
Async XLA Ops:
  7.2 58.0 %all-gather.5.cloned.1.call-start = ((), (), s32[]{:S(2)}) async-start(), calls=%async_computation.2 | async-start | bytes 5242880 | tf_op jit(solution)/shard_map/all_gather | solution.py:30
  65.1 3.4 %copy-start.1 = (bf16[1,2048,1024]{2,1,0:T(8,128)(2,1)S(1)}, bf16[1,2048,1024]{2,1,0:T(8,128)(2,1)}, u32[]{:S(2)}) copy-start(bf16[1,2048,1024]{2,1,0:T(8,128)(2,1)} %all-gather.5.cloned.1.call-done) | copy-start | bytes 12582916
  68.6 3.2 copy-start.2
  69.9 1.9 copy-start
  75.5 53.6 %all-to-all-start = ((bf16[8,512,256]{1,2,0:T(8,128)(2,1)}), bf16[8,512,256]{1,2,0:T(8,128)(2,1)S(1)}, u32[]{:S(2)}, u32[]{:S(2)}) async-start(bf16[8,512,256]{1,2,0:T(8,128)(2,1)} %convert_bitcast_fusion.1), calls=%async_computation | async-start | bytes 4194304 | tf_op jit(solution)/shard_map/all_to_all | solution.py:37
  130.9 69.1 %copy-start.3 = (f32[8,3]{0,1:T(4,128)S(1)}, f32[8,3]{0,1:T(4,128)}, u32[]{:S(2)}) copy-start(f32[8,3]{0,1:T(4,128)} %param.3) | copy-start | bytes 292
  255.0 52.6 %all-to-all-start.1 = ((bf16[8,512,256]{1,2,0:T(8,128)(2,1)}), bf16[8,512,256]{1,2,0:T(8,128)(2,1)S(1)}, u32[]{:S(2)}, u32[]{:S(2)}) async-start(bf16[8,512,256]{1,2,0:T(8,128)(2,1)} %fusion.16), calls=%async_computation.1 | async-start | bytes 4194304 | tf_op jit(solution)/shard_map/all_to_all | solution.py:47
Sparse Core Ops, SparseCore 0:
  9.8 55.2 all-gather.4
